TPU v7x, 512 devices: a whole 4x4x16 slice. The times are simulated.
512 devices in a mesh: row: 16 (over z_lo, y), mode: 32 (over z_hi, x, core).
Axes of the slice: x: 4, y: 4, z: 16 (z_hi: 4, z_lo: 4; z = z_hi * 4 + z_lo), core: 2. Of those that a mesh axis runs over, the one named last changes fastest.
Arguments:
- transfer_matrix: float32 [2, 3072, 49152], P(None, 'row', 'mode'), may hold values from -0.01953125 to 0.01953125
- probes: float32 [2, 49152, 256], P(None, ('mode', 'row')), may hold values from -6 to 6
- intensity: float32 [3072, 256], P('row'), may hold values from 0.25 to 4
Outputs:
- gradient: float32 [2, 3072, 49152], P(None, 'row', 'mode')
All inputs are finite; a program needn't handle non-finite values.
Results may differ from a plain program's by a relative error of at most 0.00012.
Values sent between devices are 32-bit elements; how exact they have to be, the bound alone decides.
A program may use at most 64 MiB of HBM per device.

v0:
```python
import jax
import jax.numpy as jnp
from jax import lax
from jax.sharding import Mesh
from jax.sharding import PartitionSpec as P

P_SIZE = 256
ROW = ("row_0", "row_1")
MODE_ROW = ("mode", "row_0", "row_1")


def joined_along(tiles, dim):
    lengths = list(tiles.shape[1:])
    lengths[dim] *= tiles.shape[0]
    return jnp.moveaxis(tiles, 0, dim).reshape(lengths)


def stacked_from(array, axes, turns):
    tiles = array[None]
    for k in turns:
        tiles = lax.all_gather(tiles, axes[k], axis=0, tiled=True)
    block = [lax.axis_size(axes[k]) for k in reversed(turns)]
    tiles = tiles.reshape(*block, *array.shape)
    turned = sorted(range(len(turns)), key=lambda place: turns[len(turns) - 1 - place])
    return tiles.transpose(*turned, *range(len(turns), tiles.ndim)).reshape(-1, *array.shape)


def whole_of(array, axes, turns, dim):
    return joined_along(stacked_from(array, axes, turns), dim)


def split_up(array, dim, count):
    before, after = (array.shape[:dim], array.shape[dim + 1 :])
    return jnp.moveaxis(array.reshape(*before, count, -1, *after), dim, 0)


def sum_at_owner(array, axis, dim):
    count = lax.axis_size(axis)
    tiles = lax.all_to_all(split_up(array, dim, count), axis, 0, 0, tiled=True)
    return jnp.sum(tiles, axis=0)


def sent_to_all(array, axis):
    count = lax.axis_size(axis)
    return lax.all_to_all(
        jnp.broadcast_to(array[None], (count, *array.shape)), axis, 0, 0, tiled=True
    )


def gather_directly(array, axis, dim):
    tiles = sent_to_all(array, axis)
    return joined_along(tiles, dim)


def exact_dot(left, right):
    return jnp.dot(left, right, precision=lax.Precision.HIGHEST, preferred_element_type=jnp.float32)


def exact_dot_transposed(left, right):
    return lax.dot_general(
        left,
        right,
        (((1,), (1,)), ((), ())),
        precision=lax.Precision.HIGHEST,
        preferred_element_type=jnp.float32,
    )


def partial_fields(matrix, strip):
    fields_real = exact_dot(matrix[0], strip[0]) - exact_dot(matrix[1], strip[1])
    fields_imag = exact_dot(matrix[0], strip[1]) + exact_dot(matrix[1], strip[0])
    return jnp.stack([fields_real, fields_imag])


def gradient_columns(residual, strip):
    grad_real = exact_dot_transposed(residual[0], strip[0]) + exact_dot_transposed(
        residual[1], strip[1]
    )
    grad_imag = exact_dot_transposed(residual[1], strip[0]) - exact_dot_transposed(
        residual[0], strip[1]
    )
    return jnp.stack([grad_real, grad_imag])


def make_residual(fields, measured):
    excess = fields[0] * fields[0] + fields[1] * fields[1] - measured
    return excess[None] * fields / P_SIZE


def body(transfer_matrix, probes, intensity):
    strip = whole_of(probes, ROW, (0, 1), 1)
    partial_value = partial_fields(transfer_matrix, strip)
    shares = sum_at_owner(partial_value, "mode", 2)
    share_width = shares.shape[2]
    measured = lax.dynamic_slice_in_dim(
        intensity, lax.axis_index("mode") * share_width, share_width, 1
    )
    residual = gather_directly(make_residual(shares, measured), "mode", 2)
    return gradient_columns(residual, strip)


def solution(mesh):
    split = Mesh(mesh.devices.reshape(4, 4, mesh.shape["mode"]), ("row_0", "row_1", "mode"))
    placed = (P(None, ROW, "mode"), P(None, MODE_ROW, None), P(ROW, None))
    return jax.shard_map(
        body, mesh=split, in_specs=placed, out_specs=P(None, ROW, "mode"), check_vma=False
    )
```

profile of v0, /device:TPU:1, one launch (start us, length us, event | category | flops | bytes accessed | tf_op | source)
XLA Modules:
  0.0 199.6 jit_solution(12416556249650519281)
XLA Ops:
  6.5 0.0 copy-start
  6.5 0.0 all-gather.3.cloned.1.call-start
  6.5 20.8 %all-gather = f32[8,96,256]{2,1,0:T(8,128)} all-gather(f32[2,96,256]{2,1,0:T(8,128)} %param.4), channel_id=2, replica_groups=mesh['row_0'=4,'row_1'=4,'mode'=32] {'row_0'}, dimensions={0}, use_global_device_ids=true | all-gather | bytes 983040 | tf_op jit(solution)/shard_map/all_gather | solution.py:21
  27.3 0.0 all-gather.3.cloned.1.call-update
  27.3 51.1 %all-gather.3.cloned.1.call-done = f32[16,2,96,256]{3,2,1,0:T(8,128)} async-done(((f32[4,2,96,256]{3,2,1,0:T(8,128)}), f32[16,2,96,256]{3,2,1,0:T(8,128)}) %all-gather.3.cloned.1.call-update) | async-done | bytes 3145744 | tf_op jit(solution)/shard_map/all_gather | solution.py:21
  78.5 2.2 %copy.11 = f32[4,4,2,96,256]{4,3,2,1,0:T(8,128)S(1)} copy(f32[4,4,2,96,256]{4,3,2,0,1:T(8,128)} %bitcast.65) | data formatting | bytes 6291456 | tf_op jit(solution)/shard_map/transpose | solution.py:25
  80.7 0.0 copy-start.1
  80.7 0.3 fusion.25
  81.0 1.3 copy-done.1
  82.4 1.2 fusion.4
  83.6 1.2 fusion.2
  84.8 1.9 fusion.10
  86.7 1.8 copy.12
  88.4 3.1 %fusion.13 = f32[192,256]{1,0:T(8,128)} fusion(f32[192,256]{1,0:T(8,128)S(1)} %fusion.2, f32[1536,256]{1,0:T(8,128)S(1)} %bitcast.57, f32[2,192,1536]{2,1,0:T(8,128)} %param.3), kind=kOutput, calls=%fused_computation.14 | convolution fusion | flops 906018816 | bytes 3145728 | tf_op jit(solution)/shard_map/dot_general | solution.py:56
  91.5 1.8 copy.13
  93.3 1.1 maximum_bitcast_fusion
  94.4 0.9 copy.14
  95.2 15.6 %all-to-all-start = ((f32[32,2,192,8]{2,3,1,0:T(8,128)}), f32[32,2,192,8]{2,3,1,0:T(8,128)}, u32[]{:S(2)}, u32[]{:S(2)}) async-start(f32[32,2,192,8]{2,3,1,0:T(8,128)} %copy.14), calls=%async_computation | async-start | bytes 1048576 | tf_op jit(solution)/shard_map/all_to_all | solution.py:39
  110.9 0.0 copy-done
  110.9 0.1 constant_dynamic-slice_fusion
  111.0 0.1 copy.18
  111.1 29.9 %all-to-all-done = f32[32,2,192,8]{2,3,1,0:T(8,128)} async-done(((f32[32,2,192,8]{2,3,1,0:T(8,128)}), f32[32,2,192,8]{2,3,1,0:T(8,128)}, u32[]{:S(2)}, u32[]{:S(2)}) %all-to-all-start) | async-done | bytes 393248 | tf_op jit(solution)/shard_map/all_to_all | solution.py:39
  141.0 1.1 reduce_sum.9
  142.1 0.1 broadcast_in_dim.5
  142.1 38.4 %all_to_all.10 = f32[32,2,192,8]{2,3,1,0:T(8,128)S(1)} all-to-all(f32[32,2,192,8]{2,3,1,0:T(8,128)S(1)} %broadcast_in_dim.5), channel_id=1, replica_groups=mesh['row_0'=4,'row_1'=4,'mode'=32] {'mode'}, dimensions={0} | all-to-all | bytes 786432 | tf_op jit(solution)/shard_map/all_to_all | solution.py:45
  180.5 2.7 %fusion.20 = f32[192,1536]{1,0:T(8,128)S(1)} fusion(f32[1536,256]{1,0:T(8,128)S(1)} %bitcast.54, f32[2,192,32,8]{1,3,0,2:T(8,128)S(1)} %bitcast.61), kind=kOutput, calls=%fused_computation.22 | convolution fusion | flops 905969664 | bytes 3014656 | tf_op jit(solution)/shard_map/dot_general | solution.py:60
  183.2 2.7 %fusion.21 = f32[192,1536]{1,0:T(8,128)S(1)} fusion(f32[1536,256]{1,0:T(8,128)S(1)} %bitcast.55, f32[2,192,32,8]{1,3,0,2:T(8,128)S(1)} %bitcast.62), kind=kOutput, calls=%fused_computation.23 | convolution fusion | flops 905969664 | bytes 3014656 | tf_op jit(solution)/shard_map/dot_general | solution.py:60
  185.9 2.7 %fusion = f32[1,192,1536]{2,1,0:T(8,128)S(1)} fusion(f32[192,1536]{1,0:T(8,128)S(1)} %fusion.20, f32[1536,256]{1,0:T(8,128)S(1)} %bitcast.58, f32[2,192,32,8]{1,3,0,2:T(8,128)S(1)} %bitcast.63), kind=kOutput, calls=%fused_computation.2 | convolution fusion | flops 906264576 | bytes 4194304 | tf_op jit(solution)/shard_map/dot_general | solution.py:60
  188.5 2.7 %fusion.1 = f32[1,192,1536]{2,1,0:T(8,128)S(1)} fusion(f32[192,1536]{1,0:T(8,128)S(1)} %fusion.21, f32[1536,256]{1,0:T(8,128)S(1)} %bitcast.59, f32[2,192,32,8]{1,3,0,2:T(8,128)S(1)} %bitcast.64), kind=kOutput, calls=%fused_computation.3 | convolution fusion | flops 906264576 | bytes 4194304 | tf_op jit(solution)/shard_map/dot_general | solution.py:60
  191.2 1.6 pad_maximum_fusion
  (2 shorter events, 0.0 us)
Async XLA Ops:
  6.5 104.4 %copy-start = (f32[192,256]{1,0:T(8,128)S(1)}, f32[192,256]{1,0:T(8,128)}, u32[]{:S(2)}) copy-start(f32[192,256]{1,0:T(8,128)} %param.5) | copy-start | bytes 589828
  6.5 71.9 %all-gather.3.cloned.1.call-start = ((), (), s32[]{:S(2)}) async-start(), calls=%async_computation.2 | async-start | bytes 3932160 | tf_op jit(solution)/shard_map/all_gather | solution.py:21
  80.7 1.7 copy-start.1
  95.2 45.7 %all-to-all-start = ((f32[32,2,192,8]{2,3,1,0:T(8,128)}), f32[32,2,192,8]{2,3,1,0:T(8,128)}, u32[]{:S(2)}, u32[]{:S(2)}) async-start(f32[32,2,192,8]{2,3,1,0:T(8,128)} %copy.14), calls=%async_computation | async-start | bytes 1048576 | tf_op jit(solution)/shard_map/all_to_all | solution.py:39
Sparse Core Ops, SparseCore 0:
  27.4 50.9 all-gather.2
where the time goes:
time: 201 us; the launch traced here: 200 us
  waiting for transfers between devices  81.1 us (40%)
  blocking collectives  59.1 us (29%)
  matrix products  18.1 us (9%)
  starting transfers between devices  15.7 us (8%)
  between operations  13.5 us (7%)
  local copies, waits for them, and re-layouts  8.45 us (4%)
  other arithmetic  3.73 us (2%)
    all_gather x1, waiting for transfers between devices, stacked_from(): tiles = lax.all_gather(tiles, axes[k], axis=0, tiled=True)  51.1 us
    all_to_all x1, blocking collectives, sent_to_all(): lax.all_to_all(jnp.broadcast_to(array[None], (count, *array.shape)), axis...  38.4 us
    all_to_all x1, waiting for transfers between devices, sum_at_owner(): tiles = lax.all_to_all(split_up(array, dim, count), axis, 0, 0, tiled=True)  29.9 us
    all_gather x1, blocking collectives, stacked_from(): tiles = lax.all_gather(tiles, axes[k], axis=0, tiled=True)  20.8 us
    all_to_all x1, starting transfers between devices, sum_at_owner(): tiles = lax.all_to_all(split_up(array, dim, count), axis, 0, 0, tiled=True)  15.6 us
    dot_general x4, matrix products, exact_dot_transposed(): lax.dot_general(left, right, (((1,), (1,)), ((), ())), precision=lax.Prec...  10.7 us
    dot_general x4, matrix products, exact_dot(): jnp.dot(left, right, precision=lax.Precision.HIGHEST, preferred_element_t...  7.41 us
  transfers between devices with their start and end apart: 2, of which 2 were waited for; matrix products, arithmetic and copies ran while one was open for 0% of the time, Pallas kernels for 0%

commit v1 on v0

v1 whole, which is shorter than its diff:
```python
import jax
import jax.numpy as jnp
from jax import lax
from jax.experimental import pallas as pl
from jax.experimental.pallas import tpu as pltpu
from jax.sharding import Mesh
from jax.sharding import PartitionSpec as P

AXES = ("zl", "y", "zh", "x", "c")
SIZES = {"zl": 4, "y": 4, "zh": 4, "x": 4, "c": 2}
CHUNKS = ((0, 128), (128, 64), (192, 64))
BY_MESH = pl.DeviceIdType.MESH
XC = tuple((dx, dc) for dx in range(4) for dc in range(2) if (dx, dc) != (0, 0))
F32, BF16 = jnp.float32, jnp.bfloat16


def shifted(axis, by):
    return lax.rem(lax.axis_index(axis) + by, SIZES[axis])


def partner(index, j):
    if j == 0:
        return index
    if j == 1:
        return index + 1 - 2 * lax.rem(index, 2)
    if j == 2:
        return lax.rem(index + 2, 4)
    return 3 - index


def halves(value):
    high = value.astype(BF16)
    return high, (value - high.astype(F32)).astype(BF16)


def dot3(a_high, a_low, b_high, b_low, contract_b):
    dims = (((1,), (contract_b,)), ((), ()))

    def dot(a, b):
        return lax.dot_general(a, b, dims, preferred_element_type=F32)

    return dot(a_high, b_high) + (dot(a_high, b_low) + dot(a_low, b_high))


def swapped(value, signs):
    width = value.shape[1] // 2
    if width % 128 == 0:
        turned = jnp.concatenate([value[:, width:], value[:, :width]], axis=1)
    else:
        turned = pltpu.roll(value, width, 1)
    return turned * signs


def sign_row(width, first, second):
    lane = lax.broadcasted_iota(jnp.int32, (1, 2 * width), 1)
    return jnp.where(lane < width, F32(first), F32(second))


def gather_kernel(
    u_hbm, s_ref, i_ref, *rest
):
    n = len(CHUNKS)
    grad, res_h, res_l, last_h, last_l = rest[:5]
    uf, uh, ul, u_sem = rest[5:9]
    per = [rest[9 + 14 * k : 9 + 14 * (k + 1)] for k in range(n)]
    zl, y, x, c = (lax.axis_index(a) for a in ("zl", "y", "x", "c"))
    own = x * 2 + c
    up, down = shifted("y", 1), shifted("y", 3)
    rows = i_ref.shape[0] // 8

    u_copy = pltpu.make_async_copy(u_hbm, uf, u_sem)
    u_copy.start()

    barrier = pltpu.get_barrier_semaphore()
    peers = [{"zl": partner(zl, j)} for j in (1, 2, 3)]
    peers += [{"y": up}, {"y": down}]
    peers += [{"x": shifted("x", dx), "c": shifted("c", dc)} for dx, dc in XC]
    peers += [{"zh": shifted("zh", d)} for d in (1, 2, 3)]
    for peer in peers:
        pl.semaphore_signal(barrier, inc=1, device_id=peer, device_id_type=BY_MESH)

    for k, (first, width) in enumerate(CHUNKS):
        strip = per[k][0]
        packed = jnp.concatenate(
            [s_ref[0, :, first : first + width], s_ref[1, :, first : first + width]], axis=1
        )
        strip[zl, y] = packed.reshape(2, 48, 2 * width)
        mine = i_ref[pl.ds(pl.multiple_of(own * rows, 8), rows), first : first + width]
        per[k][7][...] = jnp.concatenate([mine, mine], axis=1)

    pl.semaphore_wait(barrier, len(peers))

    sent = []

    def send(src, dst, send_sem, recv_sem, peer):
        copy = pltpu.make_async_remote_copy(
            src_ref=src, dst_ref=dst, send_sem=send_sem, recv_sem=recv_sem,
            device_id=peer, device_id_type=BY_MESH,
        )
        copy.start()
        sent.append(copy)
        return copy

    def issue(k):
        strip, zs, zr, ys, yr = per[k][0], *per[k][8:12]
        block = strip.at[zl, y]
        z = [
            send(block, block, zs.at[j - 1], zr.at[j - 1], {"zl": partner(zl, j)})
            for j in (1, 2, 3)
        ]
        return z, {0: both_ways(k, 0)}

    def both_ways(k, j):
        strip, ys, yr = per[k][0], per[k][10], per[k][11]
        block = strip.at[partner(zl, j), y]
        return (
            send(block, block, ys.at[j, 0], yr.at[j, 0], {"y": up}),
            send(block, block, ys.at[j, 1], yr.at[j, 1], {"y": down}),
        )

    def relay(k, j, arrivals):
        strip, ys, yr = per[k][0], per[k][10], per[k][11]
        g = partner(zl, j)
        arrivals[0].wait_recv()
        from_down = strip.at[g, down, 0]
        a = send(from_down, from_down, ys.at[j, 2], yr.at[j, 2], {"y": up})
        arrivals[1].wait_recv()
        from_up = strip.at[g, up, 1]
        b = send(from_up, from_up, ys.at[j, 3], yr.at[j, 3], {"y": down})
        return a, b

    def gather(k, started):
        z, y_copies = started
        far = {}
        for j in (0, 1, 2, 3):
            if j < 3:
                z[j].wait_recv()
                y_copies[j + 1] = both_ways(k, j + 1)
            far[j] = relay(k, j, y_copies[j])
        return far

    def fields(k, far):
        strip, sh, sl, total = per[k][:4]
        width = CHUNKS[k][1]
        for j in (0, 1, 2, 3):
            for copy in far[j]:
                copy.wait_recv()
            g = partner(zl, j)
            high, low = halves(strip[g].reshape(384, 2 * width))
            sh[g] = high
            sl[g] = low
            value = dot3(uh[g], ul[g], high, low, 0)
            if j == 0:
                total[...] = value
            else:
                total[...] += value

    def spread_fields(k):
        total, parts, got = per[k][3:6]
        width = CHUNKS[k][1]
        half = total.shape[0] // 2
        value = total[:half, :] + swapped(total[half:, :], sign_row(width, -1, 1))
        parts[...] = value.reshape(parts.shape)
        xs, xr = per[k][12].at[0], per[k][13].at[0]
        copies = []
        for i, (dx, dc) in enumerate(XC):
            tx, tc = shifted("x", dx), shifted("c", dc)
            copies.append(
                send(parts.at[tx * 2 + tc], got.at[i], xs.at[i], xr.at[i], {"x": tx, "c": tc})
            )
        return copies

    def sum_over_x(k, copies):
        parts, got, share = per[k][4], per[k][5], per[k][6]
        for copy in copies:
            copy.wait_recv()
        value = parts[own]
        for i in range(7):
            value = value + got[i]
        share[0] = value
        xs, xr = per[k][12].at[1], per[k][13].at[1]
        return [
            send(share.at[0], share.at[d], xs.at[d], xr.at[d], {"zh": shifted("zh", d)})
            for d in (1, 2, 3)
        ]

    def spread_residual(k, copies):
        parts, share, measured = per[k][4], per[k][6], per[k][7]
        got = per[k][5]
        width = CHUNKS[k][1]
        for copy in copies:
            copy.wait_recv()
        value = (share[0] + share[1]) + (share[2] + share[3])
        square = value * value
        excess = square + swapped(square, F32(1)) - measured[...]
        share[4] = excess * value * F32(1 / 256)
        gathered = per[k][3]
        place = gathered.at[pl.ds(pl.multiple_of(own * rows, 8), rows), :]
        xs, xr = per[k][12].at[2], per[k][13].at[2]
        out = []
        for i, (dx, dc) in enumerate(XC):
            peer = {"x": shifted("x", dx), "c": shifted("c", dc)}
            out.append(send(share.at[4], place, xs.at[i], xr.at[i], peer))
        gathered[pl.ds(pl.multiple_of(own * rows, 8), rows), :] = share[4]
        return out

    def residual_rows(k, copies):
        width = CHUNKS[k][1]
        for copy in copies:
            copy.wait_recv()
        value = per[k][3][: 8 * rows, :]
        stacked = jnp.concatenate([value, swapped(value, sign_row(width, 1, -1))], axis=0)
        return halves(stacked)

    def gradient(k, copies, add):
        high, low = residual_rows(k, copies)
        sh, sl = per[k][1], per[k][2]
        for g in range(4):
            value = dot3(high, low, sh[g], sl[g], 1).reshape(2, 8 * rows, 384)
            if add:
                grad[:, :, g * 384 : (g + 1) * 384] += value
            else:
                grad[:, :, g * 384 : (g + 1) * 384] = value

    started = [issue(k) for k in range(n)]

    u_copy.wait()
    for g in range(4):
        for p in range(2):
            high, low = halves(uf[p, :, g * 384 : (g + 1) * 384])
            uh[g, p * 192 : (p + 1) * 192, :] = high
            ul[g, p * 192 : (p + 1) * 192, :] = low

    fields(0, gather(0, started[0]))
    x0 = spread_fields(0)
    far1 = gather(1, started[1])
    z0 = sum_over_x(0, x0)
    fields(1, far1)
    x1 = spread_fields(1)
    far2 = gather(2, started[2])
    r0 = spread_residual(0, z0)
    z1 = sum_over_x(1, x1)
    fields(2, far2)
    x2 = spread_fields(2)
    gradient(0, r0, False)
    z2 = sum_over_x(2, x2)
    r1 = spread_residual(1, z1)
    gradient(1, r1, True)
    r2 = spread_residual(2, z2)
    last_h[...] = per[n - 1][1][...]
    last_l[...] = per[n - 1][2][...]
    high, low = residual_rows(2, r2)
    res_h[...] = high
    res_l[...] = low
    for copy in sent:
        copy.wait_send()


def finish_kernel(grad, res_h, res_l, last_h, last_l, out, done, sems):
    copies = []
    for g in range(4):
        value = dot3(res_h[...], res_l[...], last_h[g], last_l[g], 1)
        columns = pl.ds(g * 384, 384)
        done[:, :, columns] = grad[:, :, columns] + value.reshape(2, value.shape[0] // 2, 384)
        copy = pltpu.make_async_copy(done.at[:, :, columns], out.at[:, :, columns], sems.at[g])
        copy.start()
        copies.append(copy)
    for copy in copies:
        copy.wait()


def body(transfer_matrix, probes, intensity):
    _, m, cols = transfer_matrix.shape
    rows = m // 8
    width = CHUNKS[-1][1]
    vmem = pl.BlockSpec(memory_space=pltpu.VMEM)
    hbm = pl.BlockSpec(memory_space=pltpu.HBM)
    scratch = [
        pltpu.VMEM((2, m, cols), F32),
        pltpu.VMEM((4, 2 * m, cols // 4), BF16),
        pltpu.VMEM((4, 2 * m, cols // 4), BF16),
        pltpu.SemaphoreType.DMA,
    ]
    for _, w in CHUNKS:
        scratch += [
            pltpu.VMEM((4, 4, 2, 48, 2 * w), F32),
            pltpu.VMEM((4, cols // 4, 2 * w), BF16),
            pltpu.VMEM((4, cols // 4, 2 * w), BF16),
            pltpu.VMEM((2 * m, 2 * w), F32),
            pltpu.VMEM((8, rows, 2 * w), F32),
            pltpu.VMEM((7, rows, 2 * w), F32),
            pltpu.VMEM((5, rows, 2 * w), F32),
            pltpu.VMEM((rows, 2 * w), F32),
            pltpu.SemaphoreType.DMA((3,)),
            pltpu.SemaphoreType.DMA((3,)),
            pltpu.SemaphoreType.DMA((4, 4)),
            pltpu.SemaphoreType.DMA((4, 4)),
            pltpu.SemaphoreType.DMA((3, 7)),
            pltpu.SemaphoreType.DMA((3, 7)),
        ]
    outs = pl.pallas_call(
        gather_kernel,
        out_shape=(
            jax.ShapeDtypeStruct((2, m, cols), F32),
            jax.ShapeDtypeStruct((2 * m, 2 * width), BF16),
            jax.ShapeDtypeStruct((2 * m, 2 * width), BF16),
            jax.ShapeDtypeStruct((4, cols // 4, 2 * width), BF16),
            jax.ShapeDtypeStruct((4, cols // 4, 2 * width), BF16),
        ),
        in_specs=[hbm, vmem, vmem],
        out_specs=(vmem,) * 5,
        scratch_shapes=scratch,
        compiler_params=pltpu.CompilerParams(
            collective_id=0, has_side_effects=True, vmem_limit_bytes=32 * 1024 * 1024
        ),
        name="gather",
    )(transfer_matrix, probes, intensity)
    return pl.pallas_call(
        finish_kernel,
        out_shape=jax.ShapeDtypeStruct((2, m, cols), F32),
        in_specs=[vmem] * 5,
        out_specs=hbm,
        scratch_shapes=[pltpu.VMEM((2, m, cols), F32), pltpu.SemaphoreType.DMA((4,))],
        compiler_params=pltpu.CompilerParams(vmem_limit_bytes=32 * 1024 * 1024),
        name="finish",
    )(*outs)


def solution(mesh):
    split = Mesh(mesh.devices.reshape([SIZES[a] for a in AXES]), AXES)
    row, mode = ("zl", "y"), ("zh", "x", "c")
    placed = (P(None, row, mode), P(None, mode + row, None), P(row, None))
    return jax.shard_map(
        body, mesh=split, in_specs=placed, out_specs=P(None, row, mode), check_vma=False
    )
```

time: 201 us -> 83.7 us (0.42)
  waiting for transfers between devices: 81.1 us -> 0 us
  Pallas kernels: 0 us -> 78.7 us
  blocking collectives: 59.1 us -> 0 us
  matrix products: 18.1 us -> 0 us
  starting transfers between devices: 15.7 us -> 0 us
  between operations: 13.5 us -> 0.01 us
  local copies, waits for them, and re-layouts: 8.45 us -> 3.52 us
  other arithmetic: 3.73 us -> 0 us
    pallas_call x0 -> x2, Pallas kernels: none -> 78.7 us  [the longest x1 76.6 us: body(): pl.pallas_call(gather_kernel, out_shape=(jax.ShapeDtypeStruct((2, m, cols...]
    all_gather x1 -> x0, waiting for transfers between devices: 51.1 us -> none  [stacked_from(): tiles = lax.all_gather(tiles, axes[k], axis=0, tiled=True)]
    all_to_all x1 -> x0, blocking collectives: 38.4 us -> none  [sent_to_all(): lax.all_to_all(jnp.broadcast_to(array[None], (count, *array.shape)), axis...]
    all_to_all x1 -> x0, waiting for transfers between devices: 29.9 us -> none  [sum_at_owner(): tiles = lax.all_to_all(split_up(array, dim, count), axis, 0, 0, tiled=True)]
    all_gather x1 -> x0, blocking collectives: 20.8 us -> none  [stacked_from(): tiles = lax.all_gather(tiles, axes[k], axis=0, tiled=True)]
    dot_general x8 -> x0, matrix products: 18.1 us -> none  [the longest x4 10.7 us: exact_dot_transposed(): lax.dot_general(left, right, (((1,), (1,)), ((), ())), precision=lax.Prec...]
    all_to_all x1 -> x0, starting transfers between devices: 15.6 us -> none  [sum_at_owner(): tiles = lax.all_to_all(split_up(array, dim, count), axis, 0, 0, tiled=True)]
    transpose x2 -> x0, local copies, waits for them, and re-layouts: 3.07 us -> none  [the longest x1 2.22 us: stacked_from(): tiles.transpose(*turned, *range(len(turns), tiles.ndim))]
  transfers between devices with their start and end apart: 2 -> 0, of which waited for: 2 -> 0; matrix products, arithmetic and copies ran while one was open for 0% -> 0% of each run, Pallas kernels for 0% -> 0%
where the time goes in v1:
time: 83.7 us; the launch traced here: 82.3 us
  Pallas kernels  78.7 us (94%)
  local copies, waits for them, and re-layouts  3.52 us (4%)
    pallas_call x1, Pallas kernels, body(): pl.pallas_call(gather_kernel, out_shape=(jax.ShapeDtypeStruct((2, m, cols...  76.6 us
    unnamed x6, local copies, waits for them, and re-layouts  3.52 us
    pallas_call x1, Pallas kernels, body(): pl.pallas_call(finish_kernel, out_shape=jax.ShapeDtypeStruct((2, m, cols)...  2.16 us

profile of v1, /device:TPU:1, one launch (start us, length us, event | category | flops | bytes accessed | tf_op | source)
XLA Modules:
  0.0 82.3 jit_solution(6768902860273870729)
XLA Ops:
  0.0 0.0 copy-start
  0.0 1.7 %copy-done = f32[2,192,1536]{2,1,0:T(8,128)S(1)} copy-done((f32[2,192,1536]{2,1,0:T(8,128)S(1)}, f32[2,192,1536]{2,1,0:T(8,128)}, u32[]{:S(2)}) %copy-start) | copy-done | bytes 2359320
  1.7 0.0 copy-start.1
  1.7 0.9 %copy-done.1 = f32[2,96,256]{2,1,0:T(8,128)S(1)} copy-done((f32[2,96,256]{2,1,0:T(8,128)S(1)}, f32[2,96,256]{2,1,0:T(8,128)}, u32[]{:S(2)}) %copy-start.1) | copy-done | bytes 196632
  2.6 0.0 copy-start.2
  2.6 0.9 %copy-done.2 = f32[192,256]{1,0:T(8,128)S(1)} copy-done((f32[192,256]{1,0:T(8,128)S(1)}, f32[192,256]{1,0:T(8,128)}, u32[]{:S(2)}) %copy-start.2) | copy-done | bytes 196632
  3.5 76.6 %gather.1 = (f32[2,192,1536]{2,1,0:T(8,128)S(1)}, bf16[384,128]{1,0:T(8,128)(2,1)S(1)}, bf16[384,128]{1,0:T(8,128)(2,1)S(1)}, bf16[4,384,128]{2,1,0:T(8,128)(2,1)S(1)}, bf16[4,384,128]{2,1,0:T(8,128)(2,1)S(1)}) custom-call(f32[2,192,1536]{2,1,0:T(8,128)S(1)} %copy-done, f32[2,96,256]{2,1,0:T(8,128)S(1)} %copy-done.1, f32[192,256]{1,0:T(8,128)S(1)} %copy-done.2), custom_call_target="tpu_custom_call" | custom-call | tf_op jit(solution)/shard_map/gather/pallas_call | solution.py:301
  80.1 2.2 %finish.1 = f32[2,192,1536]{2,1,0:T(8,128)} custom-call(f32[2,192,1536]{2,1,0:T(8,128)S(1)} %get-tuple-element.10.grad, bf16[384,128]{1,0:T(8,128)(2,1)S(1)} %get-tuple-element.11.res_h, bf16[384,128]{1,0:T(8,128)(2,1)S(1)} %get-tuple-element.12.res_l, bf16[4,384,128]{2,1,0:T(8,128)(2,1)S(1)} %get-tuple-element.13.last_h, ...), custom_call_target="tpu_custom_call" | custom-call | tf_op jit(solution)/shard_map/finish/pallas_call | solution.py:318
Async XLA Ops:
  0.0 1.7 %copy-start = (f32[2,192,1536]{2,1,0:T(8,128)S(1)}, f32[2,192,1536]{2,1,0:T(8,128)}, u32[]{:S(2)}) copy-start(f32[2,192,1536]{2,1,0:T(8,128)} %u_hbm.1) | copy-start | bytes 7077892
  1.7 0.9 %copy-start.1 = (f32[2,96,256]{2,1,0:T(8,128)S(1)}, f32[2,96,256]{2,1,0:T(8,128)}, u32[]{:S(2)}) copy-start(f32[2,96,256]{2,1,0:T(8,128)} %s_ref.1) | copy-start | bytes 589828
  2.6 0.9 %copy-start.2 = (f32[192,256]{1,0:T(8,128)S(1)}, f32[192,256]{1,0:T(8,128)}, u32[]{:S(2)}) copy-start(f32[192,256]{1,0:T(8,128)} %i_ref.1) | copy-start | bytes 589828

commit v2 on v1

v2 whole, which is shorter than its diff:
```python
import jax
import jax.numpy as jnp
from jax import lax
from jax.experimental import pallas as pl
from jax.experimental.pallas import tpu as pltpu
from jax.sharding import Mesh
from jax.sharding import PartitionSpec as P

AXES = ("zl", "y", "zh", "x", "c")
SIZES = {"zl": 4, "y": 4, "zh": 4, "x": 4, "c": 2}
CHUNKS = ((0, 128), (128, 64), (192, 64))
BY_MESH = pl.DeviceIdType.MESH
XC = tuple((dx, dc) for dx in range(4) for dc in range(2) if (dx, dc) != (0, 0))
F32, BF16 = jnp.float32, jnp.bfloat16


def shifted(axis, by):
    return lax.rem(lax.axis_index(axis) + by, SIZES[axis])


def along_z(by):
    z = lax.rem(lax.axis_index("zh") * 4 + lax.axis_index("zl") + (by + 16), 16)
    return {"zh": lax.div(z, 4), "zl": lax.rem(z, 4)}


def partner(index, j):
    if j == 0:
        return index
    if j == 1:
        return index + 1 - 2 * lax.rem(index, 2)
    if j == 2:
        return lax.rem(index + 2, 4)
    return 3 - index


def halves(value):
    high = value.astype(BF16)
    return high, (value - high.astype(F32)).astype(BF16)


def dot3(a_high, a_low, b_high, b_low, contract_b):
    dims = (((1,), (contract_b,)), ((), ()))

    def dot(a, b):
        return lax.dot_general(a, b, dims, preferred_element_type=F32)

    return dot(a_high, b_high) + (dot(a_high, b_low) + dot(a_low, b_high))


def swapped(value, signs):
    width = value.shape[1] // 2
    if width % 128 == 0:
        turned = jnp.concatenate([value[:, width:], value[:, :width]], axis=1)
    else:
        turned = pltpu.roll(value, width, 1)
    return turned * signs


def sign_row(width, first, second):
    lane = lax.broadcasted_iota(jnp.int32, (1, 2 * width), 1)
    return jnp.where(lane < width, F32(first), F32(second))


def stacked_residual(value):
    turned = swapped(value, sign_row(value.shape[1] // 2, 1, -1))
    return halves(jnp.concatenate([value, turned], axis=0))


def gather_kernel(u_hbm, s_hbm, i_hbm, *rest):
    n = len(CHUNKS)
    grad_out, res_out, last_h, last_l = rest[:4]
    uf, uh, ul, s_ref, i_ref, grad, in_sems, out_sems, near = rest[4:13]
    per = [rest[13 + 14 * k : 13 + 14 * (k + 1)] for k in range(n)]
    zl, y, x, c = (lax.axis_index(a) for a in ("zl", "y", "x", "c"))
    own = x * 2 + c
    up, down = shifted("y", 1), shifted("y", 3)
    rows = i_ref.shape[0]
    own_rows = pl.ds(pl.multiple_of(own * rows, 8), rows)

    s_copy = pltpu.make_async_copy(s_hbm, s_ref, in_sems.at[0])
    i_copy = pltpu.make_async_copy(i_hbm.at[own_rows, :], i_ref, in_sems.at[1])
    u_copy = pltpu.make_async_copy(u_hbm, uf, in_sems.at[2])
    s_copy.start()
    i_copy.start()
    u_copy.start()

    barrier = pltpu.get_barrier_semaphore()
    peers = [{"zl": partner(zl, j)} for j in (1, 2, 3)]
    peers += [{"y": up}, {"y": down}]
    peers += [{"x": shifted("x", dx), "c": shifted("c", dc)} for dx, dc in XC]
    peers += [along_z(1), along_z(-1)]
    for peer in peers:
        pl.semaphore_signal(barrier, inc=1, device_id=peer, device_id_type=BY_MESH)

    s_copy.wait()
    i_copy.wait()
    for k, (first, width) in enumerate(CHUNKS):
        strip = per[k][0]
        packed = jnp.concatenate(
            [s_ref[0, :, first : first + width], s_ref[1, :, first : first + width]], axis=1
        )
        strip[zl * 4 + y] = packed.reshape(2, 48, 2 * width)
        mine = i_ref[:, first : first + width]
        per[k][7][...] = jnp.concatenate([mine, mine], axis=1)

    pl.semaphore_wait(barrier, len(peers))

    def announce(i):
        for by in (1 << i, -(1 << i)):
            pl.semaphore_signal(near.at[i], inc=1, device_id=along_z(by), device_id_type=BY_MESH)

    def heard(i):
        pl.semaphore_wait(near.at[i], 2)

    announce(0)

    def send(src, dst, send_sem, recv_sem, peer):
        pltpu.make_async_remote_copy(
            src_ref=src, dst_ref=dst, send_sem=send_sem, recv_sem=recv_sem,
            device_id=peer, device_id_type=BY_MESH,
        ).start()

    def await_bytes(of, sem):
        pltpu.make_async_copy(of, of, sem).wait()

    def place(j, at):
        return partner(zl, j) * 4 + at

    def both_ways(k, j):
        strip, sem, arrived = per[k][0], per[k][8], per[k][10].at[j]
        block = strip.at[place(j, y)]
        send(block, block, sem, arrived, {"y": up})
        send(block, block, sem, arrived, {"y": down})
        if direct(k, j):
            send(block, block, sem, per[k][11].at[j], {"y": shifted("y", 2)})

    def direct(k, j):
        return k == n - 1 and j == 3

    def issue(k):
        strip, sem, arrived = per[k][0], per[k][8], per[k][9]
        block = strip.at[place(0, y)]
        for j in (1, 2, 3):
            send(block, block, sem, arrived.at[j - 1], {"zl": partner(zl, j)})
        both_ways(k, 0)

    def relay(k, j):
        strip, sem, arrived = per[k][0], per[k][8], per[k][11].at[j]
        await_bytes(strip.at[pl.ds(0, 2)], per[k][10].at[j])
        if not direct(k, j):
            from_down = strip.at[place(j, down), 0]
            from_up = strip.at[place(j, up), 1]
            send(from_down, from_down, sem, arrived, {"y": up})
            send(from_up, from_up, sem, arrived, {"y": down})

    def forward(k, j):
        await_bytes(per[k][0].at[0], per[k][9].at[j - 1])
        both_ways(k, j)

    def relay_all(k):
        for j in (0, 1, 2, 3):
            relay(k, j)

    def gather(k):
        for j in (0, 1, 2, 3):
            if j < 3:
                forward(k, j + 1)
                heard(j)
                if j < 2:
                    announce(j + 1)
            relay(k, j)

    def forward_all(k):
        for j in (1, 2, 3):
            forward(k, j)

    def fields(k):
        strip, sh, sl, total = per[k][:4]
        width = CHUNKS[k][1]
        for j in (0, 1, 2, 3):
            await_bytes(strip.at[0], per[k][11].at[j])
            g = partner(zl, j)
            value = strip[pl.ds(pl.multiple_of(g * 4, 4), 4)]
            high, low = halves(value.reshape(384, 2 * width))
            sh[g] = high
            sl[g] = low
            value = dot3(uh[g], ul[g], high, low, 0)
            if j == 0:
                total[...] = value
            else:
                total[...] += value

    def spread_fields(k):
        total, parts, got = per[k][3:6]
        width = CHUNKS[k][1]
        half = total.shape[0] // 2
        value = total[:half, :] + swapped(total[half:, :], sign_row(width, -1, 1))
        parts[...] = value.reshape(parts.shape)
        for i, (dx, dc) in enumerate(XC):
            tx, tc = shifted("x", dx), shifted("c", dc)
            part = parts.at[tx * 2 + tc]
            send(part, got.at[i], per[k][12].at[0], per[k][13].at[0], {"x": tx, "c": tc})

    def sum_over_x(k):
        parts, got, share = per[k][4], per[k][5], per[k][6]
        await_bytes(got, per[k][13].at[0])
        value = parts[own]
        for i in range(7):
            value = value + got[i]
        share[0] = value
        for d in (1, 2, 3):
            peer = {"zh": shifted("zh", d)}
            send(share.at[0], share.at[d], per[k][12].at[1], per[k][13].at[1], peer)

    def spread_residual(k):
        share, measured = per[k][6], per[k][7]
        await_bytes(share.at[pl.ds(1, 3)], per[k][13].at[1])
        value = (share[0] + share[1]) + (share[2] + share[3])
        square = value * value
        excess = square + swapped(square, F32(1)) - measured[...]
        share[4] = excess * value * F32(1 / 256)
        mine = gathered(k).at[own_rows, :]
        for dx, dc in XC:
            peer = {"x": shifted("x", dx), "c": shifted("c", dc)}
            send(share.at[4], mine, per[k][12].at[2], per[k][13].at[2], peer)
        pltpu.make_async_copy(share.at[4], mine, out_sems.at[k]).start()

    def gathered(k):
        return per[k][3].at[: 8 * rows, :] if k < n - 1 else res_out

    def await_residual(k):
        await_bytes(per[k][5], per[k][13].at[2])
        await_bytes(per[k][6].at[4], out_sems.at[k])

    def gradient(k, add):
        await_residual(k)
        high, low = stacked_residual(per[k][3][: 8 * rows, :])
        sh, sl = per[k][1], per[k][2]
        for g in range(4):
            value = dot3(high, low, sh[g], sl[g], 1).reshape(2, 8 * rows, 384)
            if add:
                grad[:, :, g * 384 : (g + 1) * 384] += value
            else:
                grad[:, :, g * 384 : (g + 1) * 384] = value

    def drain(k):
        await_bytes(per[k][0].at[pl.ds(0, 15)], per[k][8])
        await_bytes(per[k][5], per[k][12].at[0])
        await_bytes(per[k][6].at[pl.ds(0, 3)], per[k][12].at[1])
        await_bytes(per[k][5], per[k][12].at[2])

    for k in range(n):
        issue(k)

    u_copy.wait()
    for g in range(4):
        for p in range(2):
            high, low = halves(uf[p, :, g * 384 : (g + 1) * 384])
            uh[g, p * 192 : (p + 1) * 192, :] = high
            ul[g, p * 192 : (p + 1) * 192, :] = low

    gather(0)
    forward_all(1)
    fields(0)
    spread_fields(0)
    relay_all(1)
    forward_all(2)
    fields(1)
    spread_fields(1)
    relay_all(2)
    sum_over_x(0)
    fields(2)
    spread_fields(2)
    keep_h = pltpu.make_async_copy(per[n - 1][1], last_h, out_sems.at[3])
    keep_l = pltpu.make_async_copy(per[n - 1][2], last_l, out_sems.at[4])
    keep_h.start()
    keep_l.start()
    sum_over_x(1)
    spread_residual(0)
    sum_over_x(2)
    spread_residual(1)
    gradient(0, False)
    gradient(1, True)
    keep_grad = pltpu.make_async_copy(grad, grad_out, out_sems.at[5])
    keep_grad.start()
    spread_residual(2)
    keep_h.wait()
    keep_l.wait()
    keep_grad.wait()
    drain(0)
    drain(1)
    drain(2)
    await_residual(2)


def finish_kernel(grad, res, last_h, last_l, out, done, sems):
    high, low = stacked_residual(res[...])
    copies = []
    for g in range(4):
        value = dot3(high, low, last_h[g], last_l[g], 1)
        columns = pl.ds(g * 384, 384)
        done[:, :, columns] = grad[:, :, columns] + value.reshape(2, value.shape[0] // 2, 384)
        copy = pltpu.make_async_copy(done.at[:, :, columns], out.at[:, :, columns], sems.at[g])
        copy.start()
        copies.append(copy)
    for copy in copies:
        copy.wait()


def body(transfer_matrix, probes, intensity):
    _, m, cols = transfer_matrix.shape
    rows = m // 8
    width = CHUNKS[-1][1]
    vmem = pl.BlockSpec(memory_space=pltpu.VMEM)
    hbm = pl.BlockSpec(memory_space=pltpu.HBM)
    scratch = [
        pltpu.VMEM((2, m, cols), F32),
        pltpu.VMEM((4, 2 * m, cols // 4), BF16),
        pltpu.VMEM((4, 2 * m, cols // 4), BF16),
        pltpu.VMEM(probes.shape, F32),
        pltpu.VMEM((rows, intensity.shape[1]), F32),
        pltpu.VMEM((2, m, cols), F32),
        pltpu.SemaphoreType.DMA((3,)),
        pltpu.SemaphoreType.DMA((6,)),
        pltpu.SemaphoreType.REGULAR((3,)),
    ]
    for _, w in CHUNKS:
        scratch += [
            pltpu.VMEM((16, 2, 48, 2 * w), F32),
            pltpu.VMEM((4, cols // 4, 2 * w), BF16),
            pltpu.VMEM((4, cols // 4, 2 * w), BF16),
            pltpu.VMEM((2 * m, 2 * w), F32),
            pltpu.VMEM((8, rows, 2 * w), F32),
            pltpu.VMEM((7, rows, 2 * w), F32),
            pltpu.VMEM((5, rows, 2 * w), F32),
            pltpu.VMEM((rows, 2 * w), F32),
            pltpu.SemaphoreType.DMA,
            pltpu.SemaphoreType.DMA((3,)),
            pltpu.SemaphoreType.DMA((4,)),
            pltpu.SemaphoreType.DMA((4,)),
            pltpu.SemaphoreType.DMA((3,)),
            pltpu.SemaphoreType.DMA((3,)),
        ]
    outs = pl.pallas_call(
        gather_kernel,
        out_shape=(
            jax.ShapeDtypeStruct((2, m, cols), F32),
            jax.ShapeDtypeStruct((m, 2 * width), F32),
            jax.ShapeDtypeStruct((4, cols // 4, 2 * width), BF16),
            jax.ShapeDtypeStruct((4, cols // 4, 2 * width), BF16),
        ),
        in_specs=[hbm] * 3,
        out_specs=(pl.BlockSpec(memory_space=pl.ANY),) * 4,
        scratch_shapes=scratch,
        compiler_params=pltpu.CompilerParams(
            collective_id=0, has_side_effects=True, vmem_limit_bytes=32 * 1024 * 1024
        ),
        name="gather",
    )(*(pltpu.with_memory_space_constraint(a, pltpu.HBM) for a in (transfer_matrix, probes, intensity)))
    return pl.pallas_call(
        finish_kernel,
        out_shape=jax.ShapeDtypeStruct((2, m, cols), F32),
        in_specs=[vmem] * 4,
        out_specs=hbm,
        scratch_shapes=[pltpu.VMEM((2, m, cols), F32), pltpu.SemaphoreType.DMA((4,))],
        compiler_params=pltpu.CompilerParams(vmem_limit_bytes=32 * 1024 * 1024),
        name="finish",
    )(*outs)


def solution(mesh):
    split = Mesh(mesh.devices.reshape([SIZES[a] for a in AXES]), AXES)
    row, mode = ("zl", "y"), ("zh", "x", "c")
    placed = (P(None, row, mode), P(None, mode + row, None), P(row, None))
    return jax.shard_map(
        body, mesh=split, in_specs=placed, out_specs=P(None, row, mode), check_vma=False
    )
```

time: 83.7 us -> 69.5 us (0.83)
  Pallas kernels: 78.7 us -> 68.3 us
  local copies, waits for them, and re-layouts: 3.52 us -> 0 us
    pallas_call x1, Pallas kernels: 76.6 us -> 66.2 us  [body(): pl.pallas_call(gather_kernel, out_shape=(jax.ShapeDtypeStruct((2, m, cols...]
    unnamed x6 -> x0, local copies, waits for them, and re-layouts: 3.52 us -> none
where the time goes in v2:
time: 69.5 us; the launch traced here: 68.3 us
  Pallas kernels  68.3 us (98%)
    pallas_call x1, Pallas kernels, body(): pl.pallas_call(gather_kernel, out_shape=(jax.ShapeDtypeStruct((2, m, cols...  66.2 us
    pallas_call x1, Pallas kernels, body(): pl.pallas_call(finish_kernel, out_shape=jax.ShapeDtypeStruct((2, m, cols)...  2.16 us

profile of v2, /device:TPU:1, one launch (start us, length us, event | category | flops | bytes accessed | tf_op | source)
XLA Modules:
  0.0 68.3 jit_solution(14482553829729934755)
XLA Ops:
  0.0 66.2 %gather.1 = (f32[2,192,1536]{2,1,0:T(8,128)S(1)}, f32[192,128]{1,0:T(8,128)S(1)}, bf16[4,384,128]{2,1,0:T(8,128)(2,1)S(1)}, bf16[4,384,128]{2,1,0:T(8,128)(2,1)S(1)}) custom-call(f32[2,192,1536]{2,1,0:T(8,128)} %u_hbm.1, f32[2,96,256]{2,1,0:T(8,128)} %s_hbm.1, f32[192,256]{1,0:T(8,128)} %i_hbm.1), custom_call_target="tpu_custom_call" | custom-call | tf_op jit(solution)/shard_map/gather/pallas_call | solution.py:344
  66.2 2.2 %finish.1 = f32[2,192,1536]{2,1,0:T(8,128)} custom-call(f32[2,192,1536]{2,1,0:T(8,128)S(1)} %get-tuple-element.9.grad, f32[192,128]{1,0:T(8,128)S(1)} %get-tuple-element.10.res, bf16[4,384,128]{2,1,0:T(8,128)(2,1)S(1)} %get-tuple-element.11.last_h, bf16[4,384,128]{2,1,0:T(8,128)(2,1)S(1)} %get-tuple-element.12.last_l), custom_call_target="tpu_custom_call" | custom-call | tf_op jit(solution)/shard_map/finish/pallas_call | solution.py:360

commit v3 on v2

--- a/solution.py
+++ b/solution.py
@@ -61,16 +61,18 @@
     return jnp.where(lane < width, F32(first), F32(second))
 
 
-def stacked_residual(value):
-    turned = swapped(value, sign_row(value.shape[1] // 2, 1, -1))
-    return halves(jnp.concatenate([value, turned], axis=0))
+def stacked_residual(value, chunks):
+    size = value.shape[1] // chunks
+    signs = sign_row(size // 2, 1, -1)
+    turned = [swapped(value[:, i * size : (i + 1) * size], signs) for i in range(chunks)]
+    return halves(jnp.concatenate([value, jnp.concatenate(turned, axis=1)], axis=0))
 
 
 def gather_kernel(u_hbm, s_hbm, i_hbm, *rest):
     n = len(CHUNKS)
-    grad_out, res_out, last_h, last_l = rest[:4]
-    uf, uh, ul, s_ref, i_ref, grad, in_sems, out_sems, near = rest[4:13]
-    per = [rest[13 + 14 * k : 13 + 14 * (k + 1)] for k in range(n)]
+    grad, res_out, last_h, last_l = rest[:4]
+    uf, uh, ul, s_ref, i_ref, sh0, sl0, in_sems, out_sems, near, b_sems = rest[4:15]
+    per = [rest[15 + 12 * k : 15 + 12 * (k + 1)] for k in range(n)]
     zl, y, x, c = (lax.axis_index(a) for a in ("zl", "y", "x", "c"))
     own = x * 2 + c
     up, down = shifted("y", 1), shifted("y", 3)
@@ -101,7 +103,7 @@
         )
         strip[zl * 4 + y] = packed.reshape(2, 48, 2 * width)
         mine = i_ref[:, first : first + width]
-        per[k][7][...] = jnp.concatenate([mine, mine], axis=1)
+        per[k][5][...] = jnp.concatenate([mine, mine], axis=1)
 
     pl.semaphore_wait(barrier, len(peers))
 
@@ -126,64 +128,99 @@
     def place(j, at):
         return partner(zl, j) * 4 + at
 
+    def part(k, at):
+        strip = per[k][0]
+        return strip.at[at] if k < n - 1 else strip.at[at, 0]
+
+    def part_half(k, at, h):
+        strip = per[k][0]
+        return strip.at[at, h] if k < n - 1 else strip.at[at, 0, pl.ds(24 * h, 24)]
+
+    def parts_like(k, count):
+        strip = per[k][0]
+        return strip.at[pl.ds(0, count)] if k < n - 1 else strip.at[pl.ds(0, count), 0]
+
     def both_ways(k, j):
-        strip, sem, arrived = per[k][0], per[k][8], per[k][10].at[j]
-        block = strip.at[place(j, y)]
+        sem, arrived = per[k][6], per[k][8].at[j]
+        block = part(k, place(j, y))
         send(block, block, sem, arrived, {"y": up})
         send(block, block, sem, arrived, {"y": down})
         if direct(k, j):
-            send(block, block, sem, per[k][11].at[j], {"y": shifted("y", 2)})
+            send(block, block, sem, per[k][9].at[j], {"y": shifted("y", 2)})
 
     def direct(k, j):
         return k == n - 1 and j == 3
 
     def issue(k):
-        strip, sem, arrived = per[k][0], per[k][8], per[k][9]
-        block = strip.at[place(0, y)]
+        sem, arrived = per[k][6], per[k][7]
+        block = part(k, place(0, y))
         for j in (1, 2, 3):
             send(block, block, sem, arrived.at[j - 1], {"zl": partner(zl, j)})
         both_ways(k, 0)
+        if k == n - 1:
+            turn(up)
+            turn(down)
+
+    def turn(to):
+        block = per[n - 1][0].at[place(0, y), 1]
+        send(block, block, per[n - 1][6], b_sems.at[0], {"y": to})
+
+    def cross():
+        strip, sem = per[n - 1][0], per[n - 1][6]
+        await_bytes(strip.at[pl.ds(0, 3), 1], b_sems.at[0])
+        column = strip.at[pl.ds(zl * 4, 4), 1]
+        for j in (1, 2, 3):
+            send(column, column, sem, b_sems.at[j], {"zl": partner(zl, j)})
 
     def relay(k, j):
-        strip, sem, arrived = per[k][0], per[k][8], per[k][11].at[j]
-        await_bytes(strip.at[pl.ds(0, 2)], per[k][10].at[j])
+        sem, arrived = per[k][6], per[k][9].at[j]
+        await_bytes(parts_like(k, 2), per[k][8].at[j])
         if not direct(k, j):
-            from_down = strip.at[place(j, down), 0]
-            from_up = strip.at[place(j, up), 1]
+            from_down = part_half(k, place(j, down), 0)
+            from_up = part_half(k, place(j, up), 1)
             send(from_down, from_down, sem, arrived, {"y": up})
             send(from_up, from_up, sem, arrived, {"y": down})
 
     def forward(k, j):
-        await_bytes(per[k][0].at[0], per[k][9].at[j - 1])
+        await_bytes(part(k, 0), per[k][7].at[j - 1])
         both_ways(k, j)
 
-    def relay_all(k):
-        for j in (0, 1, 2, 3):
+    def relay_rest(k):
+        for j in (1, 2, 3):
             relay(k, j)
 
-    def gather(k):
+    def forward_all(k):
+        for j in (1, 2, 3):
+            forward(k, j)
+
+    def gather_first():
         for j in (0, 1, 2, 3):
             if j < 3:
-                forward(k, j + 1)
+                forward(0, j + 1)
                 heard(j)
                 if j < 2:
                     announce(j + 1)
-            relay(k, j)
-
-    def forward_all(k):
-        for j in (1, 2, 3):
-            forward(k, j)
+                else:
+                    cross()
+            relay(0, j)
+            if j == 0:
+                turn(shifted("y", 2))
+            if j < 2:
+                relay(j + 1, 0)
 
     def fields(k):
-        strip, sh, sl, total = per[k][:4]
+        strip, total = per[k][:2]
         width = CHUNKS[k][1]
         for j in (0, 1, 2, 3):
-            await_bytes(strip.at[0], per[k][11].at[j])
+            await_bytes(part(k, 0), per[k][9].at[j])
+            if k == n - 1 and j > 0:
+                await_bytes(strip.at[pl.ds(0, 4), 1], b_sems.at[j])
             g = partner(zl, j)
             value = strip[pl.ds(pl.multiple_of(g * 4, 4), 4)]
             high, low = halves(value.reshape(384, 2 * width))
-            sh[g] = high
-            sl[g] = low
+            keep_high, keep_low, lanes = kept(k)
+            keep_high[g, :, lanes] = high
+            keep_low[g, :, lanes] = low
             value = dot3(uh[g], ul[g], high, low, 0)
             if j == 0:
                 total[...] = value
@@ -191,7 +228,7 @@
                 total[...] += value
 
     def spread_fields(k):
-        total, parts, got = per[k][3:6]
+        total, parts, got = per[k][1:4]
         width = CHUNKS[k][1]
         half = total.shape[0] // 2
         value = total[:half, :] + swapped(total[half:, :], sign_row(width, -1, 1))
@@ -199,22 +236,22 @@
         for i, (dx, dc) in enumerate(XC):
             tx, tc = shifted("x", dx), shifted("c", dc)
             part = parts.at[tx * 2 + tc]
-            send(part, got.at[i], per[k][12].at[0], per[k][13].at[0], {"x": tx, "c": tc})
+            send(part, got.at[i], per[k][10].at[0], per[k][11].at[0], {"x": tx, "c": tc})
 
     def sum_over_x(k):
-        parts, got, share = per[k][4], per[k][5], per[k][6]
-        await_bytes(got, per[k][13].at[0])
+        parts, got, share = per[k][2], per[k][3], per[k][4]
+        await_bytes(got, per[k][11].at[0])
         value = parts[own]
         for i in range(7):
             value = value + got[i]
         share[0] = value
         for d in (1, 2, 3):
             peer = {"zh": shifted("zh", d)}
-            send(share.at[0], share.at[d], per[k][12].at[1], per[k][13].at[1], peer)
+            send(share.at[0], share.at[d], per[k][10].at[1], per[k][11].at[1], peer)
 
     def spread_residual(k):
-        share, measured = per[k][6], per[k][7]
-        await_bytes(share.at[pl.ds(1, 3)], per[k][13].at[1])
+        share, measured = per[k][4], per[k][5]
+        await_bytes(share.at[pl.ds(1, 3)], per[k][11].at[1])
         value = (share[0] + share[1]) + (share[2] + share[3])
         square = value * value
         excess = square + swapped(square, F32(1)) - measured[...]
@@ -222,32 +259,33 @@
         mine = gathered(k).at[own_rows, :]
         for dx, dc in XC:
             peer = {"x": shifted("x", dx), "c": shifted("c", dc)}
-            send(share.at[4], mine, per[k][12].at[2], per[k][13].at[2], peer)
+            send(share.at[4], mine, per[k][10].at[2], per[k][11].at[2], peer)
         pltpu.make_async_copy(share.at[4], mine, out_sems.at[k]).start()
 
+    def kept(k):
+        if k == 0:
+            return sh0, sl0, slice(None)
+        return last_h, last_l, pl.ds(128 * (k - 1), 128)
+
     def gathered(k):
-        return per[k][3].at[: 8 * rows, :] if k < n - 1 else res_out
+        return per[0][1].at[: 8 * rows, :] if k == 0 else res_out.at[:, pl.ds(128 * (k - 1), 128)]
 
     def await_residual(k):
-        await_bytes(per[k][5], per[k][13].at[2])
-        await_bytes(per[k][6].at[4], out_sems.at[k])
-
-    def gradient(k, add):
-        await_residual(k)
-        high, low = stacked_residual(per[k][3][: 8 * rows, :])
-        sh, sl = per[k][1], per[k][2]
+        await_bytes(per[k][3], per[k][11].at[2])
+        await_bytes(per[k][4].at[4], out_sems.at[k])
+
+    def gradient_first():
+        await_residual(0)
+        high, low = stacked_residual(per[0][1][: 8 * rows, :], 1)
         for g in range(4):
-            value = dot3(high, low, sh[g], sl[g], 1).reshape(2, 8 * rows, 384)
-            if add:
-                grad[:, :, g * 384 : (g + 1) * 384] += value
-            else:
-                grad[:, :, g * 384 : (g + 1) * 384] = value
+            value = dot3(high, low, sh0[g], sl0[g], 1).reshape(2, 8 * rows, 384)
+            grad[:, :, g * 384 : (g + 1) * 384] = value
 
     def drain(k):
-        await_bytes(per[k][0].at[pl.ds(0, 15)], per[k][8])
-        await_bytes(per[k][5], per[k][12].at[0])
-        await_bytes(per[k][6].at[pl.ds(0, 3)], per[k][12].at[1])
-        await_bytes(per[k][5], per[k][12].at[2])
+        await_bytes(per[k][0].at[pl.ds(0, 15)], per[k][6])
+        await_bytes(per[k][3], per[k][10].at[0])
+        await_bytes(per[k][4].at[pl.ds(0, 3)], per[k][10].at[1])
+        await_bytes(per[k][3], per[k][10].at[2])
 
     for k in range(n):
         issue(k)
@@ -259,42 +297,32 @@
             uh[g, p * 192 : (p + 1) * 192, :] = high
             ul[g, p * 192 : (p + 1) * 192, :] = low
 
-    gather(0)
+    gather_first()
     forward_all(1)
+    forward_all(2)
     fields(0)
     spread_fields(0)
-    relay_all(1)
-    forward_all(2)
+    relay_rest(1)
+    relay_rest(2)
     fields(1)
     spread_fields(1)
-    relay_all(2)
     sum_over_x(0)
     fields(2)
     spread_fields(2)
-    keep_h = pltpu.make_async_copy(per[n - 1][1], last_h, out_sems.at[3])
-    keep_l = pltpu.make_async_copy(per[n - 1][2], last_l, out_sems.at[4])
-    keep_h.start()
-    keep_l.start()
     sum_over_x(1)
+    sum_over_x(2)
     spread_residual(0)
-    sum_over_x(2)
     spread_residual(1)
-    gradient(0, False)
-    gradient(1, True)
-    keep_grad = pltpu.make_async_copy(grad, grad_out, out_sems.at[5])
-    keep_grad.start()
+    gradient_first()
     spread_residual(2)
-    keep_h.wait()
-    keep_l.wait()
-    keep_grad.wait()
-    drain(0)
-    drain(1)
-    drain(2)
+    for k in range(n):
+        drain(k)
+    await_residual(1)
     await_residual(2)
 
 
 def finish_kernel(grad, res, last_h, last_l, out, done, sems):
-    high, low = stacked_residual(res[...])
+    high, low = stacked_residual(res[...], 2)
     copies = []
     for g in range(4):
         value = dot3(high, low, last_h[g], last_l[g], 1)
@@ -310,7 +338,7 @@
 def body(transfer_matrix, probes, intensity):
     _, m, cols = transfer_matrix.shape
     rows = m // 8
-    width = CHUNKS[-1][1]
+    width = CHUNKS[1][1] + CHUNKS[2][1]
     vmem = pl.BlockSpec(memory_space=pltpu.VMEM)
     hbm = pl.BlockSpec(memory_space=pltpu.HBM)
     scratch = [
@@ -319,16 +347,16 @@
         pltpu.VMEM((4, 2 * m, cols // 4), BF16),
         pltpu.VMEM(probes.shape, F32),
         pltpu.VMEM((rows, intensity.shape[1]), F32),
-        pltpu.VMEM((2, m, cols), F32),
+        pltpu.VMEM((4, cols // 4, 2 * CHUNKS[0][1]), BF16),
+        pltpu.VMEM((4, cols // 4, 2 * CHUNKS[0][1]), BF16),
         pltpu.SemaphoreType.DMA((3,)),
-        pltpu.SemaphoreType.DMA((6,)),
+        pltpu.SemaphoreType.DMA((3,)),
         pltpu.SemaphoreType.REGULAR((3,)),
+        pltpu.SemaphoreType.DMA((4,)),
     ]
     for _, w in CHUNKS:
         scratch += [
             pltpu.VMEM((16, 2, 48, 2 * w), F32),
-            pltpu.VMEM((4, cols // 4, 2 * w), BF16),
-            pltpu.VMEM((4, cols // 4, 2 * w), BF16),
             pltpu.VMEM((2 * m, 2 * w), F32),
             pltpu.VMEM((8, rows, 2 * w), F32),
             pltpu.VMEM((7, rows, 2 * w), F32),
@@ -350,7 +378,7 @@
             jax.ShapeDtypeStruct((4, cols // 4, 2 * width), BF16),
         ),
         in_specs=[hbm] * 3,
-        out_specs=(pl.BlockSpec(memory_space=pl.ANY),) * 4,
+        out_specs=(vmem,) * 4,
         scratch_shapes=scratch,
         compiler_params=pltpu.CompilerParams(
             collective_id=0, has_side_effects=True, vmem_limit_bytes=32 * 1024 * 1024

time: 69.5 us -> 65.5 us (0.942); the launches traced: 68.3 us -> 65.3 us
  Pallas kernels: 68.3 us -> 65.3 us
    pallas_call x1, Pallas kernels: 66.2 us -> 63.1 us  [body(): pl.pallas_call(gather_kernel, out_shape=(jax.ShapeDtypeStruct((2, m, cols...]
where the time goes in v3:
time: 65.5 us; the launch traced here: 65.3 us
  Pallas kernels  65.3 us (100%)
    pallas_call x1, Pallas kernels, body(): pl.pallas_call(gather_kernel, out_shape=(jax.ShapeDtypeStruct((2, m, cols...  63.1 us
    pallas_call x1, Pallas kernels, body(): pl.pallas_call(finish_kernel, out_shape=jax.ShapeDtypeStruct((2, m, cols)...  2.26 us

profile of v3, /device:TPU:1, one launch (start us, length us, event | category | flops | bytes accessed | tf_op | source)
XLA Modules:
  0.0 65.3 jit_solution(7206340140678002827)
XLA Ops:
  0.0 63.1 %gather.1 = (f32[2,192,1536]{2,1,0:T(8,128)S(1)}, f32[192,256]{1,0:T(8,128)S(1)}, bf16[4,384,256]{2,1,0:T(8,128)(2,1)S(1)}, bf16[4,384,256]{2,1,0:T(8,128)(2,1)S(1)}) custom-call(f32[2,192,1536]{2,1,0:T(8,128)} %u_hbm.1, f32[2,96,256]{2,1,0:T(8,128)} %s_hbm.1, f32[192,256]{1,0:T(8,128)} %i_hbm.1), custom_call_target="tpu_custom_call" | custom-call | tf_op jit(solution)/shard_map/gather/pallas_call | solution.py:372
  63.1 2.3 %finish.1 = f32[2,192,1536]{2,1,0:T(8,128)} custom-call(f32[2,192,1536]{2,1,0:T(8,128)S(1)} %get-tuple-element.9.grad, f32[192,256]{1,0:T(8,128)S(1)} %get-tuple-element.10.res, bf16[4,384,256]{2,1,0:T(8,128)(2,1)S(1)} %get-tuple-element.11.last_h, bf16[4,384,256]{2,1,0:T(8,128)(2,1)S(1)} %get-tuple-element.12.last_l), custom_call_target="tpu_custom_call" | custom-call | tf_op jit(solution)/shard_map/finish/pallas_call | solution.py:388

commit v4 on v3

--- a/solution.py
+++ b/solution.py
@@ -9,6 +9,7 @@
 AXES = ("zl", "y", "zh", "x", "c")
 SIZES = {"zl": 4, "y": 4, "zh": 4, "x": 4, "c": 2}
 CHUNKS = ((0, 128), (128, 64), (192, 64))
+FIRST_ROWS = 48
 BY_MESH = pl.DeviceIdType.MESH
 XC = tuple((dx, dc) for dx in range(4) for dc in range(2) if (dx, dc) != (0, 0))
 F32, BF16 = jnp.float32, jnp.bfloat16
@@ -38,13 +39,29 @@
     return high, (value - high.astype(F32)).astype(BF16)
 
 
-def dot3(a_high, a_low, b_high, b_low, contract_b):
+def dot(a, b, contract_b):
     dims = (((1,), (contract_b,)), ((), ()))
-
-    def dot(a, b):
-        return lax.dot_general(a, b, dims, preferred_element_type=F32)
-
-    return dot(a_high, b_high) + (dot(a_high, b_low) + dot(a_low, b_high))
+    return lax.dot_general(a, b, dims, preferred_element_type=F32)
+
+
+def fields_dot(a_high, a_low, high, low):
+    width = high.shape[1]
+    if width < 256:
+        both = dot(a_high, jnp.concatenate([high, low], axis=1), 0)
+        main, cross = both[:, :width], both[:, width:]
+    else:
+        main, cross = dot(a_high, high, 0), dot(a_high, low, 0)
+    return main + (cross + dot(a_low, high, 0))
+
+
+def gradient_dot(a_high, a_low, high, low):
+    if high.shape[1] < 256:
+        main = dot(
+            jnp.concatenate([a_high, a_low], axis=1), jnp.concatenate([high, high], axis=1), 1
+        )
+    else:
+        main = dot(a_high, high, 1) + dot(a_low, high, 1)
+    return main + dot(a_high, low, 1)
 
 
 def swapped(value, signs):
@@ -61,18 +78,16 @@
     return jnp.where(lane < width, F32(first), F32(second))
 
 
-def stacked_residual(value, chunks):
-    size = value.shape[1] // chunks
-    signs = sign_row(size // 2, 1, -1)
-    turned = [swapped(value[:, i * size : (i + 1) * size], signs) for i in range(chunks)]
-    return halves(jnp.concatenate([value, jnp.concatenate(turned, axis=1)], axis=0))
+def stacked_residual(value):
+    turned = swapped(value, sign_row(value.shape[1] // 2, 1, -1))
+    return halves(jnp.concatenate([value, turned], axis=0))
 
 
 def gather_kernel(u_hbm, s_hbm, i_hbm, *rest):
     n = len(CHUNKS)
     grad, res_out, last_h, last_l = rest[:4]
-    uf, uh, ul, s_ref, i_ref, sh0, sl0, in_sems, out_sems, near, b_sems = rest[4:15]
-    per = [rest[15 + 12 * k : 15 + 12 * (k + 1)] for k in range(n)]
+    uf, uh, ul, s_ref, i_ref, sh0, sl0, sh1, sl1, in_sems, out_sems, near, b_sems = rest[4:17]
+    per = [rest[17 + 12 * k : 17 + 12 * (k + 1)] for k in range(n)]
     zl, y, x, c = (lax.axis_index(a) for a in ("zl", "y", "x", "c"))
     own = x * 2 + c
     up, down = shifted("y", 1), shifted("y", 3)
@@ -87,10 +102,10 @@
     u_copy.start()
 
     barrier = pltpu.get_barrier_semaphore()
+    beside = [{"x": shifted("x", 1)}, {"x": shifted("x", 3)}]
+    twin = {"c": 1 - c}
     peers = [{"zl": partner(zl, j)} for j in (1, 2, 3)]
-    peers += [{"y": up}, {"y": down}]
-    peers += [{"x": shifted("x", dx), "c": shifted("c", dc)} for dx, dc in XC]
-    peers += [along_z(1), along_z(-1)]
+    peers += [{"y": up}, {"y": down}, along_z(1), along_z(-1), twin] + beside
     for peer in peers:
         pl.semaphore_signal(barrier, inc=1, device_id=peer, device_id_type=BY_MESH)
 
@@ -101,7 +116,7 @@
         packed = jnp.concatenate(
             [s_ref[0, :, first : first + width], s_ref[1, :, first : first + width]], axis=1
         )
-        strip[zl * 4 + y] = packed.reshape(2, 48, 2 * width)
+        strip[zl * 4 + y] = packed
         mine = i_ref[:, first : first + width]
         per[k][5][...] = jnp.concatenate([mine, mine], axis=1)
 
@@ -114,7 +129,15 @@
     def heard(i):
         pl.semaphore_wait(near.at[i], 2)
 
+    def announce_x(i):
+        for peer in beside + [twin][i:]:
+            pl.semaphore_signal(near.at[3 + i], inc=1, device_id=peer, device_id_type=BY_MESH)
+
+    def heard_x(i):
+        pl.semaphore_wait(near.at[3 + i], 3 - i)
+
     announce(0)
+    announce_x(0)
 
     def send(src, dst, send_sem, recv_sem, peer):
         pltpu.make_async_remote_copy(
@@ -128,17 +151,20 @@
     def place(j, at):
         return partner(zl, j) * 4 + at
 
+    def leading(k):
+        return per[k][0].shape[1] if k < n - 1 else FIRST_ROWS
+
+    trailing = pl.ds(FIRST_ROWS, per[n - 1][0].shape[1] - FIRST_ROWS)
+
     def part(k, at):
-        strip = per[k][0]
-        return strip.at[at] if k < n - 1 else strip.at[at, 0]
+        return per[k][0].at[at, pl.ds(0, leading(k))]
 
     def part_half(k, at, h):
-        strip = per[k][0]
-        return strip.at[at, h] if k < n - 1 else strip.at[at, 0, pl.ds(24 * h, 24)]
+        size = leading(k) // 2
+        return per[k][0].at[at, pl.ds(size * h, size)]
 
     def parts_like(k, count):
-        strip = per[k][0]
-        return strip.at[pl.ds(0, count)] if k < n - 1 else strip.at[pl.ds(0, count), 0]
+        return per[k][0].at[pl.ds(0, count), pl.ds(0, leading(k))]
 
     def both_ways(k, j):
         sem, arrived = per[k][6], per[k][8].at[j]
@@ -149,7 +175,7 @@
             send(block, block, sem, per[k][9].at[j], {"y": shifted("y", 2)})
 
     def direct(k, j):
-        return k == n - 1 and j == 3
+        return k == n - 1 and j > 0
 
     def issue(k):
         sem, arrived = per[k][6], per[k][7]
@@ -162,13 +188,13 @@
             turn(down)
 
     def turn(to):
-        block = per[n - 1][0].at[place(0, y), 1]
+        block = per[n - 1][0].at[place(0, y), trailing]
         send(block, block, per[n - 1][6], b_sems.at[0], {"y": to})
 
     def cross():
         strip, sem = per[n - 1][0], per[n - 1][6]
-        await_bytes(strip.at[pl.ds(0, 3), 1], b_sems.at[0])
-        column = strip.at[pl.ds(zl * 4, 4), 1]
+        await_bytes(strip.at[pl.ds(0, 3), trailing], b_sems.at[0])
+        column = strip.at[pl.ds(zl * 4, 4), trailing]
         for j in (1, 2, 3):
             send(column, column, sem, b_sems.at[j], {"zl": partner(zl, j)})
 
@@ -197,35 +223,38 @@
         for j in (0, 1, 2, 3):
             if j < 3:
                 forward(0, j + 1)
+            if j < 3:
                 heard(j)
-                if j < 2:
-                    announce(j + 1)
-                else:
-                    cross()
+            if j < 2:
+                announce(j + 1)
+            if j == 2:
+                cross()
             relay(0, j)
             if j == 0:
                 turn(shifted("y", 2))
             if j < 2:
                 relay(j + 1, 0)
-
-    def fields(k):
+                heard_x(j)
+            if j == 0:
+                announce_x(1)
+
+    def fields(k, t):
         strip, total = per[k][:2]
         width = CHUNKS[k][1]
-        for j in (0, 1, 2, 3):
+        keep_high, keep_low = kept(k)
+        for j in (2 * t, 2 * t + 1):
             await_bytes(part(k, 0), per[k][9].at[j])
             if k == n - 1 and j > 0:
-                await_bytes(strip.at[pl.ds(0, 4), 1], b_sems.at[j])
-            g = partner(zl, j)
-            value = strip[pl.ds(pl.multiple_of(g * 4, 4), 4)]
-            high, low = halves(value.reshape(384, 2 * width))
-            keep_high, keep_low, lanes = kept(k)
-            keep_high[g, :, lanes] = high
-            keep_low[g, :, lanes] = low
-            value = dot3(uh[g], ul[g], high, low, 0)
-            if j == 0:
-                total[...] = value
-            else:
-                total[...] += value
+                await_bytes(strip.at[pl.ds(0, 4), trailing], b_sems.at[j])
+        q = lax.div(zl, 2) if t == 0 else 1 - lax.div(zl, 2)
+        high, low = halves(strip[pl.ds(q * 8, 8)].reshape(768, 2 * width))
+        keep_high[q] = high
+        keep_low[q] = low
+        value = fields_dot(uh[q], ul[q], high, low)
+        if t == 0:
+            total[...] = value
+        else:
+            total[...] += value
 
     def spread_fields(k):
         total, parts, got = per[k][1:4]
@@ -263,23 +292,25 @@
         pltpu.make_async_copy(share.at[4], mine, out_sems.at[k]).start()
 
     def kept(k):
-        if k == 0:
-            return sh0, sl0, slice(None)
-        return last_h, last_l, pl.ds(128 * (k - 1), 128)
+        return ((sh0, sl0), (sh1, sl1), (last_h, last_l))[k]
 
     def gathered(k):
-        return per[0][1].at[: 8 * rows, :] if k == 0 else res_out.at[:, pl.ds(128 * (k - 1), 128)]
+        return per[k][1].at[: 8 * rows, :] if k < n - 1 else res_out
 
     def await_residual(k):
         await_bytes(per[k][3], per[k][11].at[2])
         await_bytes(per[k][4].at[4], out_sems.at[k])
 
-    def gradient_first():
-        await_residual(0)
-        high, low = stacked_residual(per[0][1][: 8 * rows, :], 1)
-        for g in range(4):
-            value = dot3(high, low, sh0[g], sl0[g], 1).reshape(2, 8 * rows, 384)
-            grad[:, :, g * 384 : (g + 1) * 384] = value
+    def gradient(k):
+        await_residual(k)
+        high, low = stacked_residual(per[k][1][: 8 * rows, :])
+        keep_high, keep_low = kept(k)
+        for q in range(2):
+            value = gradient_dot(high, low, keep_high[q], keep_low[q]).reshape(2, 8 * rows, 768)
+            if k == 0:
+                grad[:, :, q * 768 : (q + 1) * 768] = value
+            else:
+                grad[:, :, q * 768 : (q + 1) * 768] += value
 
     def drain(k):
         await_bytes(per[k][0].at[pl.ds(0, 15)], per[k][6])
@@ -291,43 +322,47 @@
         issue(k)
 
     u_copy.wait()
-    for g in range(4):
+    for q in range(2):
         for p in range(2):
-            high, low = halves(uf[p, :, g * 384 : (g + 1) * 384])
-            uh[g, p * 192 : (p + 1) * 192, :] = high
-            ul[g, p * 192 : (p + 1) * 192, :] = low
+            high, low = halves(uf[p, :, q * 768 : (q + 1) * 768])
+            uh[q, p * 192 : (p + 1) * 192, :] = high
+            ul[q, p * 192 : (p + 1) * 192, :] = low
 
     gather_first()
     forward_all(1)
-    forward_all(2)
-    fields(0)
+    fields(0, 0)
+    fields(0, 1)
     spread_fields(0)
     relay_rest(1)
+    forward_all(2)
+    fields(1, 0)
+    fields(1, 1)
+    spread_fields(1)
     relay_rest(2)
-    fields(1)
-    spread_fields(1)
     sum_over_x(0)
-    fields(2)
+    fields(2, 0)
+    fields(2, 1)
     spread_fields(2)
     sum_over_x(1)
     sum_over_x(2)
     spread_residual(0)
     spread_residual(1)
-    gradient_first()
     spread_residual(2)
+    gradient(0)
+    gradient(1)
     for k in range(n):
         drain(k)
-    await_residual(1)
     await_residual(2)
 
 
 def finish_kernel(grad, res, last_h, last_l, out, done, sems):
-    high, low = stacked_residual(res[...], 2)
+    high, low = stacked_residual(res[...])
     copies = []
-    for g in range(4):
-        value = dot3(high, low, last_h[g], last_l[g], 1)
-        columns = pl.ds(g * 384, 384)
-        done[:, :, columns] = grad[:, :, columns] + value.reshape(2, value.shape[0] // 2, 384)
+    for g in range(6):
+        of = (g // 3, pl.ds(g % 3 * 256, 256))
+        value = gradient_dot(high, low, last_h[of], last_l[of])
+        columns = pl.ds(g * 256, 256)
+        done[:, :, columns] = grad[:, :, columns] + value.reshape(2, value.shape[0] // 2, 256)
         copy = pltpu.make_async_copy(done.at[:, :, columns], out.at[:, :, columns], sems.at[g])
         copy.start()
         copies.append(copy)
@@ -338,25 +373,27 @@
 def body(transfer_matrix, probes, intensity):
     _, m, cols = transfer_matrix.shape
     rows = m // 8
-    width = CHUNKS[1][1] + CHUNKS[2][1]
+    width = CHUNKS[-1][1]
     vmem = pl.BlockSpec(memory_space=pltpu.VMEM)
     hbm = pl.BlockSpec(memory_space=pltpu.HBM)
     scratch = [
         pltpu.VMEM((2, m, cols), F32),
-        pltpu.VMEM((4, 2 * m, cols // 4), BF16),
-        pltpu.VMEM((4, 2 * m, cols // 4), BF16),
+        pltpu.VMEM((2, 2 * m, cols // 2), BF16),
+        pltpu.VMEM((2, 2 * m, cols // 2), BF16),
         pltpu.VMEM(probes.shape, F32),
         pltpu.VMEM((rows, intensity.shape[1]), F32),
-        pltpu.VMEM((4, cols // 4, 2 * CHUNKS[0][1]), BF16),
-        pltpu.VMEM((4, cols // 4, 2 * CHUNKS[0][1]), BF16),
+        pltpu.VMEM((2, cols // 2, 2 * CHUNKS[0][1]), BF16),
+        pltpu.VMEM((2, cols // 2, 2 * CHUNKS[0][1]), BF16),
+        pltpu.VMEM((2, cols // 2, 2 * CHUNKS[1][1]), BF16),
+        pltpu.VMEM((2, cols // 2, 2 * CHUNKS[1][1]), BF16),
         pltpu.SemaphoreType.DMA((3,)),
         pltpu.SemaphoreType.DMA((3,)),
-        pltpu.SemaphoreType.REGULAR((3,)),
+        pltpu.SemaphoreType.REGULAR((5,)),
         pltpu.SemaphoreType.DMA((4,)),
     ]
     for _, w in CHUNKS:
         scratch += [
-            pltpu.VMEM((16, 2, 48, 2 * w), F32),
+            pltpu.VMEM((16, cols // 16, 2 * w), F32),
             pltpu.VMEM((2 * m, 2 * w), F32),
             pltpu.VMEM((8, rows, 2 * w), F32),
             pltpu.VMEM((7, rows, 2 * w), F32),
@@ -374,8 +411,8 @@
         out_shape=(
             jax.ShapeDtypeStruct((2, m, cols), F32),
             jax.ShapeDtypeStruct((m, 2 * width), F32),
-            jax.ShapeDtypeStruct((4, cols // 4, 2 * width), BF16),
-            jax.ShapeDtypeStruct((4, cols // 4, 2 * width), BF16),
+            jax.ShapeDtypeStruct((2, cols // 2, 2 * width), BF16),
+            jax.ShapeDtypeStruct((2, cols // 2, 2 * width), BF16),
         ),
         in_specs=[hbm] * 3,
         out_specs=(vmem,) * 4,
@@ -390,7 +427,7 @@
         out_shape=jax.ShapeDtypeStruct((2, m, cols), F32),
         in_specs=[vmem] * 4,
         out_specs=hbm,
-        scratch_shapes=[pltpu.VMEM((2, m, cols), F32), pltpu.SemaphoreType.DMA((4,))],
+        scratch_shapes=[pltpu.VMEM((2, m, cols), F32), pltpu.SemaphoreType.DMA((6,))],
         compiler_params=pltpu.CompilerParams(vmem_limit_bytes=32 * 1024 * 1024),
         name="finish",
     )(*outs)

time: 65.5 us -> 64.7 us (0.988)
  Pallas kernels: 65.3 us -> 64.5 us
where the time goes in v4:
time: 64.7 us; the launch traced here: 64.5 us
  Pallas kernels  64.5 us (100%)
    pallas_call x1, Pallas kernels, body(): pl.pallas_call(gather_kernel, out_shape=(jax.ShapeDtypeStruct((2, m, cols...  62.7 us
    pallas_call x1, Pallas kernels, body(): pl.pallas_call(finish_kernel, out_shape=jax.ShapeDtypeStruct((2, m, cols)...  1.84 us

profile of v4, /device:TPU:1, one launch (start us, length us, event | category | flops | bytes accessed | tf_op | source)
XLA Modules:
  0.0 64.5 jit_solution(15182795985934926981)
XLA Ops:
  0.0 62.7 %gather.1 = (f32[2,192,1536]{2,1,0:T(8,128)S(1)}, f32[192,128]{1,0:T(8,128)S(1)}, bf16[2,768,128]{2,1,0:T(8,128)(2,1)S(1)}, bf16[2,768,128]{2,1,0:T(8,128)(2,1)S(1)}) custom-call(f32[2,192,1536]{2,1,0:T(8,128)} %u_hbm.1, f32[2,96,256]{2,1,0:T(8,128)} %s_hbm.1, f32[192,256]{1,0:T(8,128)} %i_hbm.1), custom_call_target="tpu_custom_call" | custom-call | tf_op jit(solution)/shard_map/gather/pallas_call | solution.py:409
  62.7 1.8 %finish.1 = f32[2,192,1536]{2,1,0:T(8,128)} custom-call(f32[2,192,1536]{2,1,0:T(8,128)S(1)} %get-tuple-element.9.grad, f32[192,128]{1,0:T(8,128)S(1)} %get-tuple-element.10.res, bf16[2,768,128]{2,1,0:T(8,128)(2,1)S(1)} %get-tuple-element.11.last_h, bf16[2,768,128]{2,1,0:T(8,128)(2,1)S(1)} %get-tuple-element.12.last_l), custom_call_target="tpu_custom_call" | custom-call | tf_op jit(solution)/shard_map/finish/pallas_call | solution.py:425

commit v5 on v4

--- a/solution.py
+++ b/solution.py
@@ -11,7 +11,7 @@
 CHUNKS = ((0, 128), (128, 64), (192, 64))
 FIRST_ROWS = 48
 BY_MESH = pl.DeviceIdType.MESH
-XC = tuple((dx, dc) for dx in range(4) for dc in range(2) if (dx, dc) != (0, 0))
+XC = ((2, 0), (2, 1), (1, 0), (3, 0), (1, 1), (3, 1), (0, 1))
 F32, BF16 = jnp.float32, jnp.bfloat16
 
 
@@ -175,7 +175,7 @@
             send(block, block, sem, per[k][9].at[j], {"y": shifted("y", 2)})
 
     def direct(k, j):
-        return k == n - 1 and j > 0
+        return j > (3, 2, 0)[k]
 
     def issue(k):
         sem, arrived = per[k][6], per[k][7]
@@ -274,7 +274,7 @@
         for i in range(7):
             value = value + got[i]
         share[0] = value
-        for d in (1, 2, 3):
+        for d in (2, 1, 3):
             peer = {"zh": shifted("zh", d)}
             send(share.at[0], share.at[d], per[k][10].at[1], per[k][11].at[1], peer)
 

time: 64.7 us -> 63.7 us (0.985)
  Pallas kernels: 64.5 us -> 63.5 us
    pallas_call x1, Pallas kernels: 62.7 us -> 61.7 us  [body(): pl.pallas_call(gather_kernel, out_shape=(jax.ShapeDtypeStruct((2, m, cols...]
where the time goes in v5:
time: 63.7 us; the launch traced here: 63.5 us
  Pallas kernels  63.5 us (100%)
    pallas_call x1, Pallas kernels, body(): pl.pallas_call(gather_kernel, out_shape=(jax.ShapeDtypeStruct((2, m, cols...  61.7 us
    pallas_call x1, Pallas kernels, body(): pl.pallas_call(finish_kernel, out_shape=jax.ShapeDtypeStruct((2, m, cols)...  1.84 us

profile of v5, /device:TPU:1, one launch (start us, length us, event | category | flops | bytes accessed | tf_op | source)
XLA Modules:
  0.0 63.5 jit_solution(14391089037443188152)
XLA Ops:
  0.0 61.7 %gather.1 = (f32[2,192,1536]{2,1,0:T(8,128)S(1)}, f32[192,128]{1,0:T(8,128)S(1)}, bf16[2,768,128]{2,1,0:T(8,128)(2,1)S(1)}, bf16[2,768,128]{2,1,0:T(8,128)(2,1)S(1)}) custom-call(f32[2,192,1536]{2,1,0:T(8,128)} %u_hbm.1, f32[2,96,256]{2,1,0:T(8,128)} %s_hbm.1, f32[192,256]{1,0:T(8,128)} %i_hbm.1), custom_call_target="tpu_custom_call" | custom-call | tf_op jit(solution)/shard_map/gather/pallas_call | solution.py:409
  61.7 1.8 %finish.1 = f32[2,192,1536]{2,1,0:T(8,128)} custom-call(f32[2,192,1536]{2,1,0:T(8,128)S(1)} %get-tuple-element.9.grad, f32[192,128]{1,0:T(8,128)S(1)} %get-tuple-element.10.res, bf16[2,768,128]{2,1,0:T(8,128)(2,1)S(1)} %get-tuple-element.11.last_h, bf16[2,768,128]{2,1,0:T(8,128)(2,1)S(1)} %get-tuple-element.12.last_l), custom_call_target="tpu_custom_call" | custom-call | tf_op jit(solution)/shard_map/finish/pallas_call | solution.py:425

commit v6 on v5

--- a/solution.py
+++ b/solution.py
@@ -169,10 +169,10 @@
     def both_ways(k, j):
         sem, arrived = per[k][6], per[k][8].at[j]
         block = part(k, place(j, y))
+        if direct(k, j):
+            send(block, block, sem, per[k][9].at[j], {"y": shifted("y", 2)})
         send(block, block, sem, arrived, {"y": up})
         send(block, block, sem, arrived, {"y": down})
-        if direct(k, j):
-            send(block, block, sem, per[k][9].at[j], {"y": shifted("y", 2)})
 
     def direct(k, j):
         return j > (3, 2, 0)[k]

time: 63.7 us -> 64.1 us (level)
  no operation moved by 1% of the time
where the time goes in v6:
time: 64.1 us; the launch traced here: 64 us
  Pallas kernels  64 us (100%)
    pallas_call x1, Pallas kernels, body(): pl.pallas_call(gather_kernel, out_shape=(jax.ShapeDtypeStruct((2, m, cols...  62.1 us
    pallas_call x1, Pallas kernels, body(): pl.pallas_call(finish_kernel, out_shape=jax.ShapeDtypeStruct((2, m, cols)...  1.83 us

profile of v6, /device:TPU:1, one launch (start us, length us, event | category | flops | bytes accessed | tf_op | source)
XLA Modules:
  0.0 64.0 jit_solution(3243759097271851845)
XLA Ops:
  0.0 62.1 %gather.1 = (f32[2,192,1536]{2,1,0:T(8,128)S(1)}, f32[192,128]{1,0:T(8,128)S(1)}, bf16[2,768,128]{2,1,0:T(8,128)(2,1)S(1)}, bf16[2,768,128]{2,1,0:T(8,128)(2,1)S(1)}) custom-call(f32[2,192,1536]{2,1,0:T(8,128)} %u_hbm.1, f32[2,96,256]{2,1,0:T(8,128)} %s_hbm.1, f32[192,256]{1,0:T(8,128)} %i_hbm.1), custom_call_target="tpu_custom_call" | custom-call | tf_op jit(solution)/shard_map/gather/pallas_call | solution.py:409
  62.1 1.8 %finish.1 = f32[2,192,1536]{2,1,0:T(8,128)} custom-call(f32[2,192,1536]{2,1,0:T(8,128)S(1)} %get-tuple-element.9.grad, f32[192,128]{1,0:T(8,128)S(1)} %get-tuple-element.10.res, bf16[2,768,128]{2,1,0:T(8,128)(2,1)S(1)} %get-tuple-element.11.last_h, bf16[2,768,128]{2,1,0:T(8,128)(2,1)S(1)} %get-tuple-element.12.last_l), custom_call_target="tpu_custom_call" | custom-call | tf_op jit(solution)/shard_map/finish/pallas_call | solution.py:425
